TPU v7x, 512 devices: a whole 4x8x8 slice. The times are simulated.
512 devices in a mesh: gx: 64 (over y, x, core), gz: 8 (over z).
Axes of the slice: x: 4, y: 8, z: 8, core: 2. Of those that a mesh axis runs over, the one named last changes fastest.
Arguments:
- velocity: bfloat16 [3, 32, 512, 64, 128], P(None, None, 'gx', 'gz'), may hold values from -16 to 16
- weights: float32 [512, 64, 128], P('gx', 'gz'), may hold values from 1 to 60
Outputs:
- modes: float32 [3, 32, 512, 64, 128], P(None, None, 'gx', 'gz')
All inputs are finite; a program needn't handle non-finite values.
Results may differ from a plain program's by a relative error of at most 0.0003.
Values may be sent and summed in bfloat16 or wider, within the bound.
A program may use at most 64 MiB of HBM per device.

v0:
```python
import jax
import jax.numpy as jnp
from jax import lax
from jax.sharding import PartitionSpec as P

COEFS = (0.8, -0.2, 4.0 / 105.0, -1.0 / 280.0)


def extended_2(cells, sides, width):
    for axis, dim in sides:
        count = lax.axis_size(axis)
        head = lax.slice_in_dim(cells, 0, width, axis=dim)
        tail = lax.slice_in_dim(cells, cells.shape[dim] - width, cells.shape[dim], axis=dim)
        cells = jnp.concatenate(
            [
                lax.ppermute(tail, axis, [(i, (i + 1) % count) for i in range(count)]),
                cells,
                lax.ppermute(head, axis, [((i + 1) % count, i) for i in range(count)]),
            ],
            axis=dim,
        )
    return cells


def taps(extended, axis, length):
    total = None
    for step, weight in enumerate(COEFS, start=1):
        upper = lax.slice_in_dim(extended, 4 + step, 4 + step + length, axis=axis)
        lower = lax.slice_in_dim(extended, 4 - step, 4 - step + length, axis=axis)
        term = weight * (upper - lower)
        total = term if total is None else total + term
    return total


def walled(field):
    padded = jnp.pad(field, ((0, 0), (0, 0), (0, 0), (4, 4)))
    return taps(padded, 3, field.shape[3])


def per_device(velocity, weights):
    snaps = velocity.shape[1]
    cells_x = velocity.shape[2]
    cells_z = velocity.shape[3]
    cells_y = velocity.shape[4]
    whole_ext = extended_2(velocity, (("gx", 2), ("gz", 3)), 4)
    v_stream = whole_ext[1, :, :, 4 : 4 + cells_z].astype(jnp.float32)
    w_stream = whole_ext[2, :, :, 4 : 4 + cells_z].astype(jnp.float32)
    u_span = whole_ext[0, :, 4 : 4 + cells_x].astype(jnp.float32)
    v_span = whole_ext[1, :, 4 : 4 + cells_x].astype(jnp.float32)
    inner_u = velocity[0].astype(jnp.float32)
    inner_w = velocity[2].astype(jnp.float32)
    omega_x = walled(inner_w) - taps(v_span, 2, cells_z)
    omega_y = taps(u_span, 2, cells_z) - taps(w_stream, 1, cells_x)
    omega_z = taps(v_stream, 1, cells_x) - walled(inner_u)
    vort = jnp.stack([omega_x, omega_y, omega_z])
    local_gram = lax.dot_general(
        vort * weights[None, None],
        vort,
        (((0, 2, 3, 4), (0, 2, 3, 4)), ((), ())),
        precision=lax.Precision.HIGHEST,
        preferred_element_type=jnp.float32,
    )
    factor = jnp.linalg.cholesky(lax.psum(local_gram, ("gx", "gz")))
    inverse = jax.scipy.linalg.solve_triangular(
        factor, jnp.eye(snaps, dtype=jnp.float32), lower=True
    )
    rows_all = 3 * cells_x * cells_y * cells_z * lax.axis_size("gx") * lax.axis_size("gz")
    scale_all = jnp.sqrt(jnp.float32(rows_all))
    mixed = jnp.einsum("ij,cjxzy->cixzy", inverse, vort, precision=lax.Precision.HIGHEST)
    return mixed * scale_all


def solution(mesh):
    placed = (P(None, None, "gx", "gz", None), P("gx", "gz", None))
    return jax.shard_map(
        per_device,
        mesh=mesh,
        in_specs=placed,
        out_specs=P(None, None, "gx", "gz", None),
        check_vma=False,
    )
```

profile of v0, /device:TPU:1, one launch (start us, length us, event | category | flops | bytes accessed | tf_op | source)
XLA Modules:
  0.0 188.6 jit_solution(6746897384506120188)
XLA Ops:
  0.0 2.4 %copy.3 = bf16[3,32,8,8,128]{4,1,3,2,0:T(8,128)(2,1)S(1)} copy(bf16[3,32,8,8,128]{4,3,2,1,0:T(8,128)(2,1)} %param.2) | data formatting | bytes 3145728 | tf_op args[0]
  2.8 4.6 %collective-permute-start = (bf16[3,32,4,8,128]{4,1,3,2,0:T(8,128)(2,1)S(1)}, bf16[3,32,4,8,128]{4,1,3,2,0:T(8,128)(2,1)S(1)}, u32[]{:S(2)}, u32[]{:S(2)}) collective-permute-start(bf16[3,32,4,8,128]{4,1,3,2,0:T(8,128)(2,1)S(1)} %get-tuple-element.14), channel_id=1, source_target_pairs={{0,8},{8,16},{16,24},{24,32},{32,40},{40,48},{48,56},{56,64},{64,7... | collective-permute-start | bytes 2359304 | tf_op jit(solution)/shard_map/ppermute | solution.py:16
  7.4 6.2 %collective-permute-start.1 = (bf16[3,32,4,8,128]{4,1,3,2,0:T(8,128)(2,1)S(1)}, bf16[3,32,4,8,128]{4,1,3,2,0:T(8,128)(2,1)S(1)}, u32[]{:S(2)}, u32[]{:S(2)}) collective-permute-start(bf16[3,32,4,8,128]{4,1,3,2,0:T(8,128)(2,1)S(1)} %get-tuple-element.13), channel_id=1, source_target_pairs={{8,0},{16,8},{24,16},{32,24},{40,32},{48,40},{56,48},{64,56},{72,6... | collective-permute-start | bytes 2359304 | tf_op jit(solution)/shard_map/ppermute | solution.py:18
  13.6 2.7 %collective-permute-done = bf16[3,32,4,8,128]{4,1,3,2,0:T(8,128)(2,1)S(1)} collective-permute-done((bf16[3,32,4,8,128]{4,1,3,2,0:T(8,128)(2,1)S(1)}, bf16[3,32,4,8,128]{4,1,3,2,0:T(8,128)(2,1)S(1)}, u32[]{:S(2)}, u32[]{:S(2)}) %collective-permute-start) | collective-permute-done | bytes 786464 | tf_op jit(solution)/shard_map/ppermute | solution.py:16
  16.4 1.1 constant_dynamic-update-slice_fusion.1
  17.5 3.5 %collective-permute-done.1 = bf16[3,32,4,8,128]{4,1,3,2,0:T(8,128)(2,1)S(1)} collective-permute-done((bf16[3,32,4,8,128]{4,1,3,2,0:T(8,128)(2,1)S(1)}, bf16[3,32,4,8,128]{4,1,3,2,0:T(8,128)(2,1)S(1)}, u32[]{:S(2)}, u32[]{:S(2)}) %collective-permute-start.1) | collective-permute-done | bytes 786464 | tf_op jit(solution)/shard_map/ppermute | solution.py:18
  21.1 1.0 fusion.65
  22.2 3.7 %collective-permute-start.2 = (bf16[3,32,16,4,128]{4,1,3,2,0:T(8,128)(2,1)S(1)}, bf16[3,32,16,4,128]{4,1,3,2,0:T(8,128)(2,1)S(1)}, u32[]{:S(2)}, u32[]{:S(2)}) collective-permute-start(bf16[3,32,16,4,128]{4,1,3,2,0:T(8,128)(2,1)S(1)} %get-tuple-element.7), channel_id=1, source_target_pairs={{0,1},{1,2},{2,3},{3,4},{4,5},{5,6},{6,7},{7,0},{8,9},{9,10},{10,1... | collective-permute-start | bytes 4718600 | tf_op jit(solution)/shard_map/ppermute | solution.py:16
  25.9 8.6 %collective-permute-start.3 = (bf16[3,32,16,4,128]{4,1,3,2,0:T(8,128)(2,1)S(1)}, bf16[3,32,16,4,128]{4,1,3,2,0:T(8,128)(2,1)S(1)}, u32[]{:S(2)}, u32[]{:S(2)}) collective-permute-start(bf16[3,32,16,4,128]{4,1,3,2,0:T(8,128)(2,1)S(1)} %get-tuple-element.8), channel_id=1, source_target_pairs={{1,0},{2,1},{3,2},{4,3},{5,4},{6,5},{7,6},{0,7},{9,8},{10,9},{11,1... | collective-permute-start | bytes 4718600 | tf_op jit(solution)/shard_map/ppermute | solution.py:18
  34.6 0.7 pad_convert_fusion
  35.3 0.6 fusion.33
  35.9 2.1 %fusion.10 = f32[1,32,8,8,128]{4,1,3,2,0:T(8,128)S(1)} fusion(f32[32,8,8,136]{3,0,2,1:T(8,128)S(1)} %get-tuple-element.15, f32[32,16,8,128]{3,0,2,1:T(8,128)S(1)} %get-tuple-element.10), kind=kLoop, calls=%fused_computation.12 | loop fusion | flops 6029312 | bytes 17825792 | tf_op jit(solution)/shard_map/stack | solution.py:55
  37.9 27.2 %collective-permute-done.2 = bf16[3,32,16,4,128]{4,1,3,2,0:T(8,128)(2,1)S(1)} collective-permute-done((bf16[3,32,16,4,128]{4,1,3,2,0:T(8,128)(2,1)S(1)}, bf16[3,32,16,4,128]{4,1,3,2,0:T(8,128)(2,1)S(1)}, u32[]{:S(2)}, u32[]{:S(2)}) %collective-permute-start.2) | collective-permute-done | bytes 1572896 | tf_op jit(solution)/shard_map/ppermute | solution.py:16
  65.1 0.9 collective-permute-done.3
  66.4 2.1 %fusion.27 = f32[1,32,8,8,128]{4,1,3,2,0:T(8,128)S(1)} fusion(f32[32,16,8,128]{3,0,2,1:T(8,128)S(1)} %get-tuple-element.9, f32[32,8,16,128]{3,0,2,1:T(8,128)S(1)} %get-tuple-element.6), kind=kLoop, calls=%fused_computation.38 | loop fusion | flops 6029312 | bytes 17825792 | tf_op jit(solution)/shard_map/stack | solution.py:55
  68.5 2.1 %fusion.46 = f32[1,32,8,8,128]{4,1,3,2,0:T(8,128)S(1)} fusion(f32[32,8,16,128]{3,0,2,1:T(8,128)S(1)} %get-tuple-element.5, f32[32,8,8,136]{3,0,2,1:T(8,128)S(1)} %get-tuple-element.16), kind=kLoop, calls=%fused_computation.68 | loop fusion | flops 6029312 | bytes 17825792 | tf_op jit(solution)/shard_map/stack | solution.py:55
  70.6 2.8 %fusion.4 = f32[32,32]{0,1:T(8,128)S(1)} fusion(f32[1,32,8,8,128]{4,1,3,2,0:T(8,128)S(1)} %fusion.10, f32[1,32,8,8,128]{4,1,3,2,0:T(8,128)S(1)} %fusion.27, f32[1,32,8,8,128]{4,1,3,2,0:T(8,128)S(1)} %fusion.46, f32[8,8,128]{2,1,0:T(8,128)S(1)} %copy-done.1), kind=kOutput, calls=%fused_computation.6 | convolution fusion | flops 305922048 | bytes 3182592 | tf_op jit(solution)/shard_map/dot_general | solution.py:56
  73.4 101.7 %psum.7 = f32[32,32]{0,1:T(8,128)S(1)} all-reduce(f32[32,32]{0,1:T(8,128)S(1)} %fusion.4), channel_id=1, replica_groups=mesh['gx'=64,'gz'=8] {'gx','gz'}, use_global_device_ids=true, to_apply=%region_0.1 | all-reduce | flops 1024 | bytes 8192 | tf_op jit(solution)/shard_map/psum | solution.py:63
  175.2 2.9 %cholesky.17 = f32[32,32]{1,0:T(8,128)S(1)} custom-call(f32[32,32]{1,0:T(8,128)S(1)} %fusion.62), custom_call_target="Cholesky" | custom-call | tf_op jit(solution)/shard_map/jit(cholesky)/cholesky | solution.py:63
  178.2 0.6 compare_reduce_fusion
  178.8 0.7 fusion.60
  179.5 2.4 %custom-call.7 = f32[1,32,32]{1,2,0:T(8,128)S(1)} custom-call(f32[1,32,32]{2,1,0:T(8,128)S(1)} %fusion.60), custom_call_target="InvertDiagBlocksLowerTriangular" | custom-call | tf_op jit(solution)/shard_map/jit(_solve_triangular)/triangular_solve | solution.py:64
  182.1 3.0 %multiply_bitcast_fusion = f32[3,32,8,8,128]{4,1,3,2,0:T(8,128)S(1)} fusion(f32[32,32,1,1,1]{1,0,4,3,2:T(8,128)S(1)} %convolution_bitcast_fusion, f32[1,32,8,8,128]{4,1,3,2,0:T(8,128)S(1)} %fusion.10, f32[1,32,8,8,128]{4,1,3,2,0:T(8,128)S(1)} %fusion.27, f32[1,32,8,8,128]{4,1,3,2,0:T(8,128)S(1)} %fusion.46), kind=kOutput, calls=%fused_computation.3 | convolution fusion | flops 304349184 | bytes 6295552 | tf_op jit(solution)/shard_map/ij,cjxzy->cixzy/dot_general | solution.py:69
  185.1 3.5 %copy.10 = f32[3,32,8,8,128]{4,3,2,1,0:T(8,128)} copy(f32[3,32,8,8,128]{4,1,3,2,0:T(8,128)S(1)} %multiply_bitcast_fusion) | data formatting | bytes 6291456 | tf_op jit(solution)/shard_map/mul | solution.py:70
  (13 shorter events, 1.2 us)
Async XLA Ops:
  2.4 14.0 %copy-start = (bf16[3,32,8,8,128]{4,3,2,1,0:T(8,128)(2,1)S(1)}, bf16[3,32,8,8,128]{4,3,2,1,0:T(8,128)(2,1)}, u32[]{:S(2)}) copy-start(bf16[3,32,8,8,128]{4,3,2,1,0:T(8,128)(2,1)} %param.2) | copy-start | bytes 4718596
  2.8 13.6 %collective-permute-start = (bf16[3,32,4,8,128]{4,1,3,2,0:T(8,128)(2,1)S(1)}, bf16[3,32,4,8,128]{4,1,3,2,0:T(8,128)(2,1)S(1)}, u32[]{:S(2)}, u32[]{:S(2)}) collective-permute-start(bf16[3,32,4,8,128]{4,1,3,2,0:T(8,128)(2,1)S(1)} %get-tuple-element.14), channel_id=1, source_target_pairs={{0,8},{8,16},{16,24},{24,32},{32,40},{40,48},{48,56},{56,64},{64,7... | collective-permute-start | bytes 2359304 | tf_op jit(solution)/shard_map/ppermute | solution.py:16
  7.4 13.6 %collective-permute-start.1 = (bf16[3,32,4,8,128]{4,1,3,2,0:T(8,128)(2,1)S(1)}, bf16[3,32,4,8,128]{4,1,3,2,0:T(8,128)(2,1)S(1)}, u32[]{:S(2)}, u32[]{:S(2)}) collective-permute-start(bf16[3,32,4,8,128]{4,1,3,2,0:T(8,128)(2,1)S(1)} %get-tuple-element.13), channel_id=1, source_target_pairs={{8,0},{16,8},{24,16},{32,24},{40,32},{48,40},{56,48},{64,56},{72,6... | collective-permute-start | bytes 2359304 | tf_op jit(solution)/shard_map/ppermute | solution.py:18
  22.2 43.0 %collective-permute-start.2 = (bf16[3,32,16,4,128]{4,1,3,2,0:T(8,128)(2,1)S(1)}, bf16[3,32,16,4,128]{4,1,3,2,0:T(8,128)(2,1)S(1)}, u32[]{:S(2)}, u32[]{:S(2)}) collective-permute-start(bf16[3,32,16,4,128]{4,1,3,2,0:T(8,128)(2,1)S(1)} %get-tuple-element.7), channel_id=1, source_target_pairs={{0,1},{1,2},{2,3},{3,4},{4,5},{5,6},{6,7},{7,0},{8,9},{9,10},{10,1... | collective-permute-start | bytes 4718600 | tf_op jit(solution)/shard_map/ppermute | solution.py:16
  25.9 40.1 %collective-permute-start.3 = (bf16[3,32,16,4,128]{4,1,3,2,0:T(8,128)(2,1)S(1)}, bf16[3,32,16,4,128]{4,1,3,2,0:T(8,128)(2,1)S(1)}, u32[]{:S(2)}, u32[]{:S(2)}) collective-permute-start(bf16[3,32,16,4,128]{4,1,3,2,0:T(8,128)(2,1)S(1)} %get-tuple-element.8), channel_id=1, source_target_pairs={{1,0},{2,1},{3,2},{4,3},{5,4},{6,5},{7,6},{0,7},{9,8},{10,9},{11,1... | collective-permute-start | bytes 4718600 | tf_op jit(solution)/shard_map/ppermute | solution.py:18
  68.5 2.1 %copy-start.1 = (f32[8,8,128]{2,1,0:T(8,128)S(1)}, f32[8,8,128]{2,1,0:T(8,128)}, u32[]{:S(2)}) copy-start(f32[8,8,128]{2,1,0:T(8,128)} %param.3) | copy-start | bytes 98308
where the time goes:
time: 189 us
  blocking collectives  102 us (54%)
  waiting for transfers between devices  34.3 us (18%)
  starting transfers between devices  23.1 us (12%)
  other arithmetic  14.6 us (8%)
  local copies, waits for them, and re-layouts  8.7 us (5%)
  matrix products  6.01 us (3%)
    psum x1, blocking collectives, per_device(): factor = jnp.linalg.cholesky(lax.psum(local_gram, ('gx', 'gz')))  102 us
    ppermute x2, waiting for transfers between devices, extended_2(): lax.ppermute(tail, axis, [(i, (i + 1) % count) for i in range(count)])  29.9 us
    ppermute x2, starting transfers between devices, extended_2(): lax.ppermute(head, axis, [((i + 1) % count, i) for i in range(count)])  14.8 us
    ppermute x2, starting transfers between devices, extended_2(): lax.ppermute(tail, axis, [(i, (i + 1) % count) for i in range(count)])  8.35 us
    another operation x3, other arithmetic, per_device(): vort = jnp.stack([omega_x, omega_y, omega_z])  6.27 us
    ppermute x2, waiting for transfers between devices, extended_2(): lax.ppermute(head, axis, [((i + 1) % count, i) for i in range(count)])  4.41 us
  transfers between devices with their start and end apart: 4, of which 4 were waited for; matrix products, arithmetic and copies ran while one was open for 2% of the time, Pallas kernels for 0%

commit v1 on v0

v1 whole, which is shorter than its diff:
```python
import functools

import jax
import jax.numpy as jnp
from jax import lax
from jax.experimental import pallas as pl
from jax.experimental.pallas import tpu as pltpu
from jax.sharding import PartitionSpec as P

COEFS = (0.8, -0.2, 4.0 / 105.0, -1.0 / 280.0)
MESH = pl.DeviceIdType.MESH
F32 = jnp.float32
BF16 = jnp.bfloat16
PAIR = 2
CHUNKS = 4
U, V, W = 0, 1, 2


def groups_of(count):
    low = 8 if count % 8 == 0 else 2
    return low, count // low


def dot_nt(a, b):
    return lax.dot_general(a, b, (((1,), (1,)), ((), ())), preferred_element_type=F32)


def dot_nn(a, b):
    return lax.dot_general(a, b, (((1,), (0,)), ((), ())), preferred_element_type=F32)


def combine(upper_of, lower_of):
    total = None
    for step, weight in enumerate(COEFS, start=1):
        term = weight * (upper_of(step) - lower_of(step))
        total = term if total is None else total + term
    return total


def along_lanes(field):
    rows, lanes = field.shape
    lane = lax.broadcasted_iota(jnp.int32, (rows, lanes), 1)

    def upper(step):
        return jnp.where(lane < lanes - step, pltpu.roll(field, lanes - step, 1), 0.0)

    def lower(step):
        return jnp.where(lane >= step, pltpu.roll(field, step, 1), 0.0)

    return combine(upper, lower)


def along_sublanes(inner, halo):
    count, cells, lanes = inner.shape
    row = lax.broadcasted_iota(jnp.int32, (count, cells, lanes), 1)

    def upper(step):
        return pltpu.roll(jnp.where(row < step, halo, inner), cells - step, 1)

    def lower(step):
        return pltpu.roll(jnp.where(row >= cells - step, halo, inner), step, 1)

    return combine(upper, lower)


def gram_kernel(
    axes,
    vel_hbm,
    weights_ref,
    gram_ref,
    high_hbm,
    low_hbm,
    vel,
    halo_x,
    halo_z,
    part,
    high,
    low,
    acc,
    slots,
    vel_sem,
    x_send,
    x_recv,
    z_send,
    z_recv,
    slot_send,
    slot_recv,
    out_sem,
):
    snaps, cells_x, cells_z, cells_y = vel_hbm.shape[1:]
    count_x, count_z = axes
    low_count, high_count = groups_of(count_x)
    gx, gz = lax.axis_index("gx"), lax.axis_index("gz")
    near, far = lax.rem(gx, low_count), gx // low_count
    right_x, left_x = lax.rem(gx + 1, count_x), lax.rem(gx + count_x - 1, count_x)
    right_z, left_z = lax.rem(gz + 1, count_z), lax.rem(gz + count_z - 1, count_z)
    width = 4

    loads = [
        pltpu.make_async_copy(vel_hbm.at[c], vel.at[c], vel_sem.at[c]) for c in range(3)
    ]
    for load in loads:
        load.start()

    phases = (
        (count_z, gz, lambda q: (gx, q)),
        (low_count, near, lambda q: (far * low_count + q, gz)),
        (high_count, far, lambda q: (q * low_count + near, gz)),
    )

    barrier = pltpu.get_barrier_semaphore()
    total_signals = 2
    for peer in ((right_x, gz), (left_x, gz)):
        pl.semaphore_signal(barrier, inc=1, device_id=peer, device_id_type=MESH)
    for count, place, peer_of in phases:
        for d in range(1, count):
            pl.semaphore_signal(
                barrier, inc=1, device_id=peer_of(lax.rem(place + d, count)), device_id_type=MESH
            )
            total_signals += 1
    pl.semaphore_wait(barrier, total_signals)

    planes = cells_x // CHUNKS
    z_copies = {}
    x_copies = {}

    def start_z(k):
        source = (V, U)[k]
        for chunk in range(CHUNKS):
            xs = pl.ds(chunk * planes, planes)
            for side, peer in ((0, (gx, left_z)), (1, (gx, right_z))):
                rows = pl.ds(side * width, width)
                copy = pltpu.make_async_remote_copy(
                    src_ref=vel_hbm.at[source, :, xs, rows, :],
                    dst_ref=halo_z.at[k, :, xs, rows, :],
                    send_sem=z_send.at[k, chunk, side],
                    recv_sem=z_recv.at[k, chunk, side],
                    device_id=peer,
                    device_id_type=MESH,
                )
                copy.start()
                z_copies[k, chunk, side] = copy

    def start_x():
        for k, source in enumerate((V, W)):
            for side, peer, first in ((0, (right_x, gz), cells_x - width), (1, (left_x, gz), 0)):
                copy = pltpu.make_async_remote_copy(
                    src_ref=vel_hbm.at[source, :, pl.ds(first, width)],
                    dst_ref=halo_x.at[k, side],
                    send_sem=x_send.at[k, side],
                    recv_sem=x_recv.at[k, side],
                    device_id=peer,
                    device_id_type=MESH,
                )
                copy.start()
                x_copies[k, side] = copy

    start_x()
    start_z(0)
    start_z(1)

    for load in loads:
        load.wait()

    rows_pair = PAIR * cells_z

    @pl.loop(0, snaps)
    def _(s):
        for k, source in enumerate((W, U)):
            field = vel[source, s].astype(F32).reshape(cells_x * cells_z, cells_y)
            part[k, s] = along_lanes(field).reshape(cells_x, cells_z, cells_y)

    root = jnp.sqrt(weights_ref[...])

    def keep(c, i, first, value):
        for x in range(value.shape[1]):
            scaled = (value[:, x] * root[first + x][None]).reshape(rows_pair, cells_y)
            rounded = scaled.astype(BF16)
            rows = pl.ds(pl.multiple_of(i * rows_pair, rows_pair), rows_pair)
            high[c, first + x, rows, :] = rounded
            low[c, first + x, rows, :] = (scaled - rounded.astype(F32)).astype(BF16)

    def accumulate(c, first, count):
        tops = [high[c, first + x] for x in range(count)]
        rests = [low[c, first + x] for x in range(count)]
        left = jnp.concatenate(tops + tops + rests, axis=1)
        right = jnp.concatenate(tops + rests + tops, axis=1)
        acc[...] += dot_nt(left, right)

    acc[...] = jnp.zeros_like(acc)

    def stream(k, pair):
        ext = jnp.concatenate(
            [
                halo_x[k, 0, pair].astype(F32),
                vel[(V, W)[k], pair].astype(F32),
                halo_x[k, 1, pair].astype(F32),
            ],
            axis=1,
        )
        return combine(
            lambda step: ext[:, width + step : width + step + cells_x],
            lambda step: ext[:, width - step : width - step + cells_x],
        )

    for side in range(2):
        x_copies[0, side].wait_recv()

    @pl.loop(0, snaps // PAIR)
    def _(i):
        pair = pl.ds(i * PAIR, PAIR)
        keep(2, i, 0, stream(0, pair) - part[1, pair])

    for side in range(2):
        x_copies[1, side].wait_recv()

    @pl.loop(0, snaps // PAIR)
    def _(i):
        pair = pl.ds(i * PAIR, PAIR)
        part[1, pair] = stream(1, pair)

    for chunk in range(CHUNKS):
        accumulate(2, chunk * planes, planes)

    outs = []

    def send_out(c):
        for n, (source, target) in enumerate(((high, high_hbm), (low, low_hbm))):
            copy = pltpu.make_async_copy(source.at[c], target.at[c], out_sem.at[n, c])
            copy.start()
            outs.append(copy)

    send_out(2)

    for k, source in enumerate((V, U)):
        for chunk in range(CHUNKS):
            first = chunk * planes
            xs = pl.ds(first, planes)
            for side in range(2):
                z_copies[k, chunk, side].wait_recv()

            @pl.loop(0, snaps // PAIR)
            def _(i):
                pair = pl.ds(i * PAIR, PAIR)
                inner = vel[source, pair, xs].astype(F32)
                beside = halo_z[k, pair, xs].astype(F32)
                shape = inner.shape
                flat = (PAIR * planes, cells_z, cells_y)
                span = along_sublanes(inner.reshape(flat), beside.reshape(flat)).reshape(shape)
                other = part[k, pair, xs]
                keep(k, i, first, other - span if k == 0 else span - other)

            accumulate(k, first, planes)
        send_out(k)

    size = snaps * cells_z
    square = acc[...].reshape(snaps, cells_z, size)
    row = lax.broadcasted_iota(jnp.int32, square.shape, 1)
    column = lax.broadcasted_iota(jnp.int32, square.shape, 2)
    matched = jnp.where(row == lax.rem(column, cells_z), square, 0.0).sum(axis=1)
    lanes = gram_ref.shape[1]
    place_row = lax.broadcasted_iota(jnp.int32, (size, lanes), 0)
    place_col = lax.broadcasted_iota(jnp.int32, (size, lanes), 1)
    packed = None
    per_row = gram_ref.shape[0]
    for q in range(snaps // per_row):
        gather = (place_row // cells_z + q * snaps == place_col).astype(BF16)
        piece = matched[q * per_row : (q + 1) * per_row]
        one = piece.astype(BF16)
        rest = piece - one.astype(F32)
        two = rest.astype(BF16)
        three = (rest - two.astype(F32)).astype(BF16)
        term = dot_nn(one, gather) + dot_nn(two, gather) + dot_nn(three, gather)
        packed = term if packed is None else packed + term

    slot_copies = []
    value = packed
    for phase, (count, place, peer_of) in enumerate(phases):
        slots[phase, place] = value
        waits = []
        for d in range(1, count):
            q = lax.rem(place + d, count)
            copy = pltpu.make_async_remote_copy(
                src_ref=slots.at[phase, place],
                dst_ref=slots.at[phase, place],
                send_sem=slot_send.at[phase, d],
                recv_sem=slot_recv.at[phase, place],
                device_id=peer_of(q),
                device_id_type=MESH,
            )
            copy.start()
            slot_copies.append(copy)
            waits.append(
                pltpu.make_async_remote_copy(
                    src_ref=slots.at[phase, q],
                    dst_ref=slots.at[phase, q],
                    send_sem=slot_send.at[phase, d],
                    recv_sem=slot_recv.at[phase, q],
                    device_id=peer_of(q),
                    device_id_type=MESH,
                )
            )
        for copy in waits:
            copy.wait_recv()
        terms = [slots[phase, j] for j in range(count)]
        while len(terms) > 1:
            terms = [sum(terms[j + 1 : j + 2], terms[j]) for j in range(0, len(terms), 2)]
        value = terms[0]
    gram_ref[...] = value

    for copy in slot_copies:
        copy.wait_send()
    for copy in x_copies.values():
        copy.wait_send()
    for copy in z_copies.values():
        copy.wait_send()
    for copy in outs:
        copy.wait()


def gram_call(axes, velocity, weights):
    _, snaps, cells_x, cells_z, cells_y = velocity.shape
    size = snaps * cells_z
    held = jax.ShapeDtypeStruct((3, cells_x, size, cells_y), BF16)
    dma = pltpu.SemaphoreType.DMA
    most = 8
    return pl.pallas_call(
        functools.partial(gram_kernel, axes),
        out_shape=(jax.ShapeDtypeStruct((8, 128), F32), held, held),
        in_specs=[
            pl.BlockSpec(memory_space=pl.ANY),
            pl.BlockSpec(memory_space=pltpu.VMEM),
        ],
        out_specs=(
            pl.BlockSpec(memory_space=pltpu.VMEM),
            pl.BlockSpec(memory_space=pl.ANY),
            pl.BlockSpec(memory_space=pl.ANY),
        ),
        scratch_shapes=[
            pltpu.VMEM(velocity.shape, BF16),
            pltpu.VMEM((2, 2, snaps, 4, cells_z, cells_y), BF16),
            pltpu.VMEM((2, snaps, cells_x, cells_z, cells_y), BF16),
            pltpu.VMEM((2, snaps, cells_x, cells_z, cells_y), F32),
            pltpu.VMEM(held.shape, BF16),
            pltpu.VMEM(held.shape, BF16),
            pltpu.VMEM((size, size), F32),
            pltpu.VMEM((3, most, 8, 128), F32),
            dma((3,)),
            dma((2, 2)),
            dma((2, 2)),
            dma((2, CHUNKS, 2)),
            dma((2, CHUNKS, 2)),
            dma((3, most)),
            dma((3, most)),
            dma((2, 3)),
        ],
        compiler_params=pltpu.CompilerParams(
            collective_id=0, has_side_effects=True, vmem_limit_bytes=28 << 20
        ),
        name="curl_gram",
    )(velocity, weights)


def mix_kernel(
    scale, gram_ref, weights_ref, high_hbm, low_hbm, out_hbm, high, low, out, in_sem, out_sem
):
    _, cells_x, size, cells_y = high.shape
    snaps = out.shape[1]
    cells_z = size // snaps
    loads = []
    for c in range(3):
        for n, (source, target) in enumerate(((high_hbm, high), (low_hbm, low))):
            copy = pltpu.make_async_copy(source.at[c], target.at[c], in_sem.at[n, c])
            copy.start()
            loads.append(copy)

    packed = gram_ref[...]
    lanes = packed.shape[1]
    lane = lax.broadcasted_iota(jnp.int32, (snaps, lanes), 1)
    row = lax.broadcasted_iota(jnp.int32, (snaps, lanes), 0)
    pieces = [packed] + [
        pltpu.roll(packed, lanes - q * snaps, 1) for q in range(1, lanes // snaps)
    ]
    work = jnp.concatenate(pieces, axis=0)
    work = jnp.where(lane < snaps, work, jnp.where(lane == row + snaps, 1.0, 0.0))
    for k in range(snaps - 1):
        pivot = work[k : k + 1]
        column = work[:, k : k + 1] / work[k : k + 1, k : k + 1]
        work = work - jnp.where(row > k, column, 0.0) * pivot
    diagonal = jnp.where(lane == row, work, 0.0).sum(axis=1, keepdims=True)
    work = jnp.where((lane >= snaps) & (lane < 2 * snaps), work, 0.0) / jnp.sqrt(diagonal)

    spread_row = lax.broadcasted_iota(jnp.int32, (lanes, size), 0)
    spread_col = lax.broadcasted_iota(jnp.int32, (lanes, size), 1)
    spread = (spread_row == snaps + spread_col // cells_z).astype(BF16)
    top = work.astype(BF16)
    rest = (work - top.astype(F32)).astype(BF16)
    cube = (snaps, cells_z, size)
    match = lax.broadcasted_iota(jnp.int32, cube, 1) == lax.rem(
        lax.broadcasted_iota(jnp.int32, cube, 2), cells_z
    )

    def blocks(matrix):
        wide = jnp.broadcast_to(dot_nn(matrix, spread)[:, None], cube)
        return jnp.where(match, wide, 0.0).reshape(size, size).astype(BF16)

    top, rest = blocks(top), blocks(rest)
    left = jnp.concatenate([top, top, rest], axis=1)
    unscale = scale / jnp.sqrt(weights_ref[...])

    for load in loads:
        load.wait()
    stores = []
    for c in range(3):
        for x in range(0, cells_x, 2):
            a = jnp.concatenate([high[c, x], high[c, x + 1]], axis=1)
            b = jnp.concatenate([low[c, x], low[c, x + 1]], axis=1)
            mixed = dot_nn(left, jnp.concatenate([a, b, a], axis=0))
            for n in range(2):
                cut = mixed[:, n * cells_y : (n + 1) * cells_y]
                out[c, :, x + n] = cut.reshape(snaps, cells_z, cells_y) * unscale[x + n][None]
        copy = pltpu.make_async_copy(out.at[c], out_hbm.at[c], out_sem.at[c])
        copy.start()
        stores.append(copy)
    for copy in stores:
        copy.wait()


def mix_call(scale, shape, gram, weights, high, low):
    dma = pltpu.SemaphoreType.DMA
    return pl.pallas_call(
        functools.partial(mix_kernel, scale),
        out_shape=jax.ShapeDtypeStruct(shape, F32),
        in_specs=[
            pl.BlockSpec(memory_space=pltpu.VMEM),
            pl.BlockSpec(memory_space=pltpu.VMEM),
            pl.BlockSpec(memory_space=pl.ANY),
            pl.BlockSpec(memory_space=pl.ANY),
        ],
        out_specs=pl.BlockSpec(memory_space=pl.ANY),
        scratch_shapes=[
            pltpu.VMEM(high.shape, BF16),
            pltpu.VMEM(low.shape, BF16),
            pltpu.VMEM(shape, F32),
            dma((2, 3)),
            dma((3,)),
        ],
        compiler_params=pltpu.CompilerParams(vmem_limit_bytes=28 << 20),
        name="mix",
    )(gram, weights, high, low)


def solution(mesh):
    placed = (P(None, None, "gx", "gz", None), P("gx", "gz", None))
    axes = (mesh.shape["gx"], mesh.shape["gz"])

    def per_device(velocity, weights):
        rows_all = 3 * weights.size * axes[0] * axes[1]
        scale = float(rows_all) ** 0.5
        gram, high, low = gram_call(axes, velocity, weights)
        return mix_call(scale, velocity.shape, gram, weights, high, low)

    return jax.shard_map(
        per_device,
        mesh=mesh,
        in_specs=placed,
        out_specs=P(None, None, "gx", "gz", None),
        check_vma=False,
    )
```

time: 189 us -> 52 us (0.28)
  blocking collectives: 102 us -> 0 us
  Pallas kernels: 0 us -> 49.6 us
  waiting for transfers between devices: 34.3 us -> 0 us
  starting transfers between devices: 23.1 us -> 0 us
  other arithmetic: 14.6 us -> 0 us
  local copies, waits for them, and re-layouts: 8.7 us -> 2.16 us
  matrix products: 6.01 us -> 0 us
    psum x1 -> x0, blocking collectives: 102 us -> none  [per_device(): factor = jnp.linalg.cholesky(lax.psum(local_gram, ('gx', 'gz')))]
    pallas_call x0 -> x2, Pallas kernels: none -> 49.6 us  [the longest x1 44.2 us: gram_call(): pl.pallas_call(functools.partial(gram_kernel, axes), out_shape=(jax.Shape...]
    ppermute x4 -> x0, waiting for transfers between devices: 34.3 us -> none  [the longest x2 29.9 us: extended_2(): lax.ppermute(tail, axis, [(i, (i + 1) % count) for i in range(count)])]
    ppermute x4 -> x0, starting transfers between devices: 23.1 us -> none  [the longest x2 14.8 us: extended_2(): lax.ppermute(head, axis, [((i + 1) % count, i) for i in range(count)])]
    another operation x8 -> x0, other arithmetic: 13 us -> none  [the longest x3 6.27 us: per_device(): vort = jnp.stack([omega_x, omega_y, omega_z])]
    dot_general x2 -> x0, matrix products: 5.79 us -> none  [the longest x1 2.98 us: per_device(): jnp.einsum('ij,cjxzy->cixzy', inverse, vort, precision=lax.Precision.HIGH...]
    mul x1 -> x0, local copies, waits for them, and re-layouts: 3.49 us -> none  [per_device(): return mixed * scale_all]
  transfers between devices with their start and end apart: 4 -> 0, of which waited for: 4 -> 0; matrix products, arithmetic and copies ran while one was open for 2% -> 0% of each run, Pallas kernels for 0% -> 0%
where the time goes in v1:
time: 52 us; the launch traced here: 51.8 us
  Pallas kernels  49.6 us (95%)
  local copies, waits for them, and re-layouts  2.16 us (4%)
    pallas_call x1, Pallas kernels, gram_call(): pl.pallas_call(functools.partial(gram_kernel, axes), out_shape=(jax.Shape...  44.2 us
    pallas_call x1, Pallas kernels, mix_call(): pl.pallas_call(functools.partial(mix_kernel, scale), out_shape=jax.ShapeD...  5.42 us
    unnamed x4, local copies, waits for them, and re-layouts  2.16 us

profile of v1, /device:TPU:1, one launch (start us, length us, event | category | flops | bytes accessed | tf_op | source)
XLA Modules:
  0.0 51.8 jit_solution(11876959636618176187)
XLA Ops:
  0.0 0.0 copy-start
  0.0 1.4 %copy-done = bf16[3,32,8,8,128]{4,3,2,1,0:T(8,128)(2,1)S(1)} copy-done((bf16[3,32,8,8,128]{4,3,2,1,0:T(8,128)(2,1)S(1)}, bf16[3,32,8,8,128]{4,3,2,1,0:T(8,128)(2,1)}, u32[]{:S(2)}) %copy-start) | copy-done | bytes 1572888
  1.4 0.0 copy-start.1
  1.4 0.8 %copy-done.1 = f32[8,8,128]{2,1,0:T(8,128)S(1)} copy-done((f32[8,8,128]{2,1,0:T(8,128)S(1)}, f32[8,8,128]{2,1,0:T(8,128)}, u32[]{:S(2)}) %copy-start.1) | copy-done | bytes 32792
  2.2 44.2 %curl_gram.1 = (f32[8,128]{1,0:T(8,128)S(1)}, bf16[3,8,256,128]{3,2,1,0:T(8,128)(2,1)S(1)}, bf16[3,8,256,128]{3,2,1,0:T(8,128)(2,1)S(1)}) custom-call(bf16[3,32,8,8,128]{4,3,2,1,0:T(8,128)(2,1)S(1)} %copy-done, f32[8,8,128]{2,1,0:T(8,128)S(1)} %copy-done.1), custom_call_target="tpu_custom_call" | custom-call | tf_op jit(solution)/shard_map/curl_gram/pallas_call | solution.py:327
  46.4 5.4 %mix.1 = f32[3,32,8,8,128]{4,3,2,1,0:T(8,128)} custom-call(f32[8,128]{1,0:T(8,128)S(1)} %get-tuple-element.8.gram_ref, f32[8,8,128]{2,1,0:T(8,128)S(1)} %copy-done.1, bf16[3,8,256,128]{3,2,1,0:T(8,128)(2,1)S(1)} %get-tuple-element.9.high_hbm, bf16[3,8,256,128]{3,2,1,0:T(8,128)(2,1)S(1)} %get-tuple-element.10.low_hbm), custom_call_target="tpu_custom_call" | custom-call | tf_op jit(solution)/shard_map/mix/pallas_call | solution.py:431
Async XLA Ops:
  0.0 1.4 %copy-start = (bf16[3,32,8,8,128]{4,3,2,1,0:T(8,128)(2,1)S(1)}, bf16[3,32,8,8,128]{4,3,2,1,0:T(8,128)(2,1)}, u32[]{:S(2)}) copy-start(bf16[3,32,8,8,128]{4,3,2,1,0:T(8,128)(2,1)} %vel_hbm.1) | copy-start | bytes 4718596
  1.4 0.8 %copy-start.1 = (f32[8,8,128]{2,1,0:T(8,128)S(1)}, f32[8,8,128]{2,1,0:T(8,128)}, u32[]{:S(2)}) copy-start(f32[8,8,128]{2,1,0:T(8,128)} %weights_ref.3) | copy-start | bytes 98308

commit v2 on v0

v2 whole, which is shorter than its diff:
```python
import functools
import itertools

import jax
import jax.numpy as jnp
from jax import lax
from jax.experimental import pallas as pl
from jax.experimental.pallas import tpu as pltpu
from jax.sharding import PartitionSpec as P

WHOLE = 840.0
COEFS = (672.0, -168.0, 32.0, -3.0)
WIDTH = len(COEFS)
MESH = pl.DeviceIdType.MESH
F32 = jnp.float32
BF16 = jnp.bfloat16
PAIR = 2
U, V, W = 0, 1, 2


def dims_of(count_x, count_z):
    core = 2
    x = 4 if count_x % 8 == 0 else 1
    return {"y": count_x // (core * x), "x": x, "core": core, "z": count_z}


PHASES = (("y", "core"), ("z", "x"))


def offsets_of(names, dims):
    def hops(offset):
        return sum(
            min(d, dims[n] - d) * (0.1 if n == "core" else 1.0)
            for n, d in zip(names, offset, strict=True)
        )

    every = itertools.product(*[range(dims[n]) for n in names])
    return sorted((o for o in every if any(o)), key=lambda o: -hops(o))


def dot_nt(a, b):
    return lax.dot_general(a, b, (((1,), (1,)), ((), ())), preferred_element_type=F32)


def dot_nn(a, b):
    return lax.dot_general(a, b, (((1,), (0,)), ((), ())), preferred_element_type=F32)


def stencil(distance):
    total = jnp.zeros(distance.shape, F32)
    for step, weight in enumerate(COEFS, start=1):
        total = jnp.where(distance == step, weight, total)
        total = jnp.where(distance == -step, -weight, total)
    return total


def iota(shape, dim):
    return lax.broadcasted_iota(jnp.int32, shape, dim)


def gram_kernel(
    axes,
    scale,
    vel_hbm,
    weights_hbm,
    gram_ref,
    high,
    low,
    unscale,
    vel,
    weights,
    halo_x,
    halo_z,
    part,
    span_matrix,
    acc,
    slots,
    vel_sem,
    x_send,
    x_recv,
    z_send,
    z_recv,
    slot_send,
    slot_recv,
):
    snaps, cells_x, cells_z, cells_y = vel_hbm.shape[1:]
    size = snaps * cells_z
    count_x, count_z = axes
    dims = dims_of(count_x, count_z)
    gx, gz = lax.axis_index("gx"), lax.axis_index("gz")
    core_x = dims["x"] * dims["core"]
    mine = {
        "y": gx // core_x,
        "x": lax.rem(gx // dims["core"], dims["x"]),
        "core": lax.rem(gx, dims["core"]),
        "z": gz,
    }

    def peer_at(names, offset):
        place = dict(mine)
        for name, d in zip(names, offset, strict=True):
            if d:
                place[name] = lax.rem(place[name] + d, dims[name])
        return (place["y"] * core_x + place["x"] * dims["core"] + place["core"], place["z"])

    right_x, left_x = lax.rem(gx + 1, count_x), lax.rem(gx + count_x - 1, count_x)
    right_z, left_z = lax.rem(gz + 1, count_z), lax.rem(gz + count_z - 1, count_z)

    barrier = pltpu.get_barrier_semaphore()
    announced = [(right_x, gz), (left_x, gz), (gx, right_z), (gx, left_z)]
    for names in PHASES:
        announced += [peer_at(names, offset) for offset in offsets_of(names, dims)]
    for peer in announced:
        pl.semaphore_signal(barrier, inc=1, device_id=peer, device_id_type=MESH)

    loads = [
        pltpu.make_async_copy(vel_hbm.at[c], vel.at[c], vel_sem.at[c]) for c in (W, U, V)
    ]
    loads.append(pltpu.make_async_copy(weights_hbm, weights, vel_sem.at[3]))
    for load in loads:
        load.start()

    pl.semaphore_wait(barrier, len(announced))

    z_copies = {}
    x_copies = {}

    def start_z(k):
        source = (V, U)[k]
        for first in range(0, cells_x, 2):
            xs = pl.ds(first, 2)
            for side, peer in ((0, (gx, left_z)), (1, (gx, right_z))):
                rows = pl.ds(side * WIDTH, WIDTH)
                copy = pltpu.make_async_remote_copy(
                    src_ref=vel_hbm.at[source, :, xs, rows, :],
                    dst_ref=halo_z.at[k, :, xs, rows, :],
                    send_sem=z_send.at[k, first // 2, side],
                    recv_sem=z_recv.at[k, first // 2, side],
                    device_id=peer,
                    device_id_type=MESH,
                )
                copy.start()
                z_copies[k, first, side] = copy

    def start_x():
        for k, source in enumerate((V, W)):
            for side, peer, first in ((0, (right_x, gz), cells_x - WIDTH), (1, (left_x, gz), 0)):
                copy = pltpu.make_async_remote_copy(
                    src_ref=vel_hbm.at[source, :, pl.ds(first, WIDTH)],
                    dst_ref=halo_x.at[k, side],
                    send_sem=x_send.at[k, side],
                    recv_sem=x_recv.at[k, side],
                    device_id=peer,
                    device_id_type=MESH,
                )
                copy.start()
                x_copies[k, side] = copy

    start_z(0)
    start_x()
    start_z(1)

    wall = stencil(iota((cells_y, cells_y), 0) - iota((cells_y, cells_y), 1)).astype(BF16)
    wide = (size, size)
    to_row, from_row = iota(wide, 0), iota(wide, 1)
    same = to_row // cells_z == from_row // cells_z
    to_z, from_z = lax.rem(to_row, cells_z), lax.rem(from_row, cells_z)
    beyond = jnp.where(from_z < WIDTH, from_z + cells_z, from_z - cells_z)
    for n, source_z in enumerate((from_z, beyond)):
        span_matrix[:, n * size : (n + 1) * size] = jnp.where(
            same, stencil(source_z - to_z), 0.0
        ).astype(BF16)
    acc[...] = jnp.zeros_like(acc)

    for load in loads:
        load.wait()

    root_weights = jnp.sqrt(weights[...])
    root = root_weights * (1.0 / WHOLE)
    unscale[...] = scale / root_weights

    def plane_of(ref, c, x):
        return ref[c, :, x].reshape(size, cells_y)

    @pl.loop(0, cells_x)
    def _(x):
        both = jnp.concatenate([plane_of(vel, W, x), plane_of(vel, U, x)], axis=0)
        part[pl.ds(0, 2), x] = dot_nn(both, wall).reshape(2, size, cells_y)

    def keep(c, x, rows, value):
        scaled = (value.reshape(-1, cells_z, cells_y) * root[x][None]).reshape(value.shape)
        rounded = scaled.astype(BF16)
        high[c, x, rows, :] = rounded
        low[c, x, rows, :] = (scaled - rounded.astype(F32)).astype(BF16)

    def accumulate(c, first, count):
        tops = jnp.concatenate([high[c, first + x] for x in range(count)], axis=1)
        rests = jnp.concatenate([low[c, first + x] for x in range(count)], axis=1)
        acc[...] += dot_nt(jnp.concatenate([tops, rests], axis=0), tops)

    rows_pair = PAIR * cells_z

    def stream(k, i):
        pair = pl.ds(i * PAIR, PAIR)
        ext = jnp.concatenate(
            [
                halo_x[k, 0, pair].astype(F32),
                vel[(V, W)[k], pair].astype(F32),
                halo_x[k, 1, pair].astype(F32),
            ],
            axis=1,
        )
        for x in range(cells_x):
            total = None
            for step, weight in enumerate(COEFS, start=1):
                term = weight * (ext[:, WIDTH + x + step] - ext[:, WIDTH + x - step])
                total = term if total is None else total + term
            yield x, total.reshape(rows_pair, cells_y)

    for side in range(2):
        x_copies[0, side].wait_recv()

    @pl.loop(0, snaps // PAIR)
    def _(i):
        rows = pl.ds(pl.multiple_of(i * rows_pair, rows_pair), rows_pair)
        for x, value in stream(0, i):
            keep(2, x, rows, value - part[1, x, rows])

    for side in range(2):
        x_copies[1, side].wait_recv()

    @pl.loop(0, snaps // PAIR)
    def _(i):
        rows = pl.ds(pl.multiple_of(i * rows_pair, rows_pair), rows_pair)
        for x, value in stream(1, i):
            part[1, x, rows] = value

    for first in range(0, cells_x, 4):
        accumulate(2, first, 4)

    for k, source in enumerate((V, U)):
        for first in range(0, cells_x, 2):
            for side in range(2):
                z_copies[k, first, side].wait_recv()
            xs = (first, first + 1)
            inner = jnp.concatenate([plane_of(vel, source, x) for x in xs], axis=1)
            beside = jnp.concatenate([plane_of(halo_z, k, x) for x in xs], axis=1)
            span = dot_nn(span_matrix[...], jnp.concatenate([inner, beside], axis=0))
            for n, x in enumerate(xs):
                cut = span[:, n * cells_y : (n + 1) * cells_y]
                keep(k, x, slice(None), part[0, x] - cut if k == 0 else cut - part[1, x])
            accumulate(k, first, 2)

    square = acc[...].reshape(2 * snaps, cells_z, size)
    match = iota(square.shape, 1) == lax.rem(iota(square.shape, 2), cells_z)
    matched = jnp.where(match, square, 0.0).sum(axis=1)
    matched = 0.5 * matched[:snaps] + matched[snaps:]
    per_row, lanes = gram_ref.shape
    gather = (iota((size, lanes), 0) // cells_z == iota((size, lanes), 1)).astype(BF16)
    one = matched.astype(BF16)
    rest = matched - one.astype(F32)
    two = rest.astype(BF16)
    three = (rest - two.astype(F32)).astype(BF16)
    half = dot_nn(jnp.concatenate([one, two, three], axis=0), gather)
    half = half[:snaps] + half[snaps : 2 * snaps] + half[2 * snaps :]
    packed = half[:per_row]
    for q in range(1, snaps // per_row):
        packed += pltpu.roll(half[q * per_row : (q + 1) * per_row], q * snaps, 1)

    slot_copies = []
    value = packed
    base = 0
    for phase, names in enumerate(PHASES):
        offsets = offsets_of(names, dims)
        slots[base] = value
        for n, offset in enumerate(offsets, start=1):
            pltpu.make_async_remote_copy(
                src_ref=slots.at[base],
                dst_ref=slots.at[base + n],
                send_sem=slot_send.at[phase],
                recv_sem=slot_recv.at[phase],
                device_id=peer_at(names, offset),
                device_id_type=MESH,
            ).start()
        landed = slots.at[pl.ds(base + 1, len(offsets))]
        everything = pltpu.make_async_remote_copy(
            src_ref=landed,
            dst_ref=landed,
            send_sem=slot_send.at[phase],
            recv_sem=slot_recv.at[phase],
            device_id=peer_at(names, offsets[0]),
            device_id_type=MESH,
        )
        everything.wait_recv()
        slot_copies.append(everything)
        terms = [slots[base + n] for n in range(len(offsets) + 1)]
        while len(terms) > 1:
            terms = [sum(terms[j + 1 : j + 2], terms[j]) for j in range(0, len(terms), 2)]
        value = terms[0]
        base += len(offsets) + 1
    gram_ref[...] = value

    for copy in slot_copies:
        copy.wait_send()
    for copy in x_copies.values():
        copy.wait_send()
    for copy in z_copies.values():
        copy.wait_send()


def gram_call(axes, scale, velocity, weights):
    _, snaps, cells_x, cells_z, cells_y = velocity.shape
    size = snaps * cells_z
    held = jax.ShapeDtypeStruct((3, cells_x, size, cells_y), BF16)
    dma = pltpu.SemaphoreType.DMA
    dims = dims_of(*axes)
    tiles = sum(len(offsets_of(names, dims)) + 1 for names in PHASES)
    return pl.pallas_call(
        functools.partial(gram_kernel, axes, scale),
        out_shape=(
            jax.ShapeDtypeStruct((8, 128), F32),
            held,
            held,
            jax.ShapeDtypeStruct(weights.shape, F32),
        ),
        in_specs=[pl.BlockSpec(memory_space=pltpu.HBM)] * 2,
        out_specs=(pl.BlockSpec(memory_space=pltpu.VMEM),) * 4,
        scratch_shapes=[
            pltpu.VMEM(velocity.shape, BF16),
            pltpu.VMEM(weights.shape, F32),
            pltpu.VMEM((2, 2, snaps, WIDTH, cells_z, cells_y), BF16),
            pltpu.VMEM((2, snaps, cells_x, cells_z, cells_y), BF16),
            pltpu.VMEM((2, cells_x, size, cells_y), F32),
            pltpu.VMEM((size, 2 * size), BF16),
            pltpu.VMEM((2 * size, size), F32),
            pltpu.VMEM((tiles, 8, 128), F32),
            dma((4,)),
            dma((2, 2)),
            dma((2, 2)),
            dma((2, cells_x // 2, 2)),
            dma((2, cells_x // 2, 2)),
            dma((len(PHASES),)),
            dma((len(PHASES),)),
        ],
        compiler_params=pltpu.CompilerParams(
            collective_id=0, has_side_effects=True, vmem_limit_bytes=28 << 20
        ),
        name="curl_gram",
    )(velocity, weights)


BLOCK = 8


def eliminate(gram):
    snaps, lanes = gram.shape
    tile = 8
    lane = iota((tile, lanes), 1)
    row = iota((tile, lanes), 0)
    full = (tile, lanes)
    work = []
    for t in range(snaps // tile):
        unit = jnp.where(lane == row + snaps + t * tile, 1.0, 0.0)
        work.append(jnp.where(lane < snaps, gram[t * tile : (t + 1) * tile], unit))
    roots = [jnp.ones(full, F32) for _ in work]
    for b in range(0, snaps, BLOCK):
        steps = range(BLOCK)
        home, at = b // tile, [(b + j) % tile for j in steps]
        rows = [jnp.broadcast_to(work[home][at[j] : at[j] + 1], full) for j in steps]
        columns = [
            {
                t: jnp.broadcast_to(work[t][:, b + j : b + j + 1], full)
                for t in range(home, len(work))
            }
            for j in steps
        ]
        cross = [
            [jnp.broadcast_to(columns[j][home][at[i] : at[i] + 1], full) for j in steps]
            for i in steps
        ]
        for j in steps:
            pivot = cross[j][j]
            inverse = 1.0 / pivot
            roots[home] = jnp.where(row == at[j], pivot, roots[home])
            factors = {t: columns[j][t] * inverse for t in columns[j]}
            factors[home] = jnp.where(row > at[j], factors[home], 0.0)
            for m in steps[j + 1 :]:
                for t in columns[m]:
                    columns[m][t] = columns[m][t] - factors[t] * cross[j][m]
            for i in steps[j + 1 :]:
                ratio = cross[i][j] * inverse
                rows[i] = rows[i] - ratio * rows[j]
                for m in steps[j + 1 :]:
                    cross[i][m] = cross[i][m] - ratio * cross[j][m]
            for t in columns[j]:
                work[t] = work[t] - factors[t] * rows[j]
    return jnp.concatenate([w / jnp.sqrt(r) for w, r in zip(work, roots, strict=True)], axis=0)


def mix_kernel(gram_ref, unscale, high, low, out_hbm, out, out_sem):
    _, cells_x, size, cells_y = high.shape
    snaps = out.shape[1]
    cells_z = size // snaps

    packed = gram_ref[...]
    lanes = packed.shape[1]
    pieces = [packed] + [
        pltpu.roll(packed, lanes - q * snaps, 1) for q in range(1, lanes // snaps)
    ]
    half = jnp.concatenate(pieces, axis=0)
    half = jnp.where(iota(half.shape, 1) < snaps, half, 0.0)
    tall = jnp.concatenate([half, jnp.zeros((lanes - snaps, lanes), F32)], axis=0)
    inverse = eliminate(half + tall.T[:snaps])
    place = iota(inverse.shape, 1)
    inverse = jnp.where((place >= snaps) & (place < 2 * snaps), inverse, 0.0)

    spread = (iota((lanes, size), 0) == snaps + iota((lanes, size), 1) // cells_z).astype(BF16)
    top = inverse.astype(BF16)
    rest = (inverse - top.astype(F32)).astype(BF16)
    spans = dot_nn(jnp.concatenate([top, rest], axis=0), spread)
    cube = (2 * snaps, cells_z, size)
    match = iota(cube, 1) == lax.rem(iota(cube, 2), cells_z)
    left = jnp.where(match, jnp.broadcast_to(spans[:, None], cube), 0.0)
    left = left.reshape(2 * size, size).astype(BF16)

    stores = []
    for c in range(3):
        for first in range(0, cells_x, 2):
            xs = (first, first + 1)
            a = jnp.concatenate([high[c, x] for x in xs], axis=1)
            b = jnp.concatenate([low[c, x] for x in xs], axis=1)
            mixed = dot_nn(left, a)
            mixed = mixed[:size] + mixed[size:] + dot_nn(left[:size], b)
            for n, x in enumerate(xs):
                cut = mixed[:, n * cells_y : (n + 1) * cells_y]
                out[c, :, x] = cut.reshape(snaps, cells_z, cells_y) * unscale[x][None]
            where = (c, slice(None), pl.ds(first, 2))
            copy = pltpu.make_async_copy(
                out.at[where], out_hbm.at[where], out_sem.at[c, first // 2]
            )
            copy.start()
            stores.append(copy)
    for copy in stores:
        copy.wait()


def mix_call(shape, gram, unscale, high, low):
    return pl.pallas_call(
        mix_kernel,
        out_shape=jax.ShapeDtypeStruct(shape, F32),
        in_specs=[pl.BlockSpec(memory_space=pltpu.VMEM)] * 4,
        out_specs=pl.BlockSpec(memory_space=pltpu.HBM),
        scratch_shapes=[
            pltpu.VMEM(shape, F32),
            pltpu.SemaphoreType.DMA((3, shape[2] // 2)),
        ],
        compiler_params=pltpu.CompilerParams(vmem_limit_bytes=28 << 20),
        name="mix",
    )(gram, unscale, high, low)


def solution(mesh):
    placed = (P(None, None, "gx", "gz", None), P("gx", "gz", None))
    axes = (mesh.shape["gx"], mesh.shape["gz"])

    def per_device(velocity, weights):
        rows_all = 3 * weights.size * axes[0] * axes[1]
        scale = float(rows_all) ** 0.5
        velocity, weights = (
            pltpu.with_memory_space_constraint(a, pltpu.HBM) for a in (velocity, weights)
        )
        gram, high, low, unscale = gram_call(axes, scale, velocity, weights)
        return mix_call(velocity.shape, gram, unscale, high, low)

    return jax.shard_map(
        per_device,
        mesh=mesh,
        in_specs=placed,
        out_specs=P(None, None, "gx", "gz", None),
        check_vma=False,
    )
```

time: 189 us -> 45.4 us (0.24)
  blocking collectives: 102 us -> 0 us
  Pallas kernels: 0 us -> 45.3 us
  waiting for transfers between devices: 34.3 us -> 0 us
  starting transfers between devices: 23.1 us -> 0 us
  other arithmetic: 14.6 us -> 0 us
  local copies, waits for them, and re-layouts: 8.7 us -> 0 us
  matrix products: 6.01 us -> 0 us
    psum x1 -> x0, blocking collectives: 102 us -> none  [per_device(): factor = jnp.linalg.cholesky(lax.psum(local_gram, ('gx', 'gz')))]
    pallas_call x0 -> x2, Pallas kernels: none -> 45.3 us  [the longest x1 41.7 us: gram_call(): pl.pallas_call(functools.partial(gram_kernel, axes, scale), out_shape=(ja...]
    ppermute x4 -> x0, waiting for transfers between devices: 34.3 us -> none  [the longest x2 29.9 us: extended_2(): lax.ppermute(tail, axis, [(i, (i + 1) % count) for i in range(count)])]
    ppermute x4 -> x0, starting transfers between devices: 23.1 us -> none  [the longest x2 14.8 us: extended_2(): lax.ppermute(head, axis, [((i + 1) % count, i) for i in range(count)])]
    another operation x8 -> x0, other arithmetic: 13 us -> none  [the longest x3 6.27 us: per_device(): vort = jnp.stack([omega_x, omega_y, omega_z])]
    dot_general x2 -> x0, matrix products: 5.79 us -> none  [the longest x1 2.98 us: per_device(): jnp.einsum('ij,cjxzy->cixzy', inverse, vort, precision=lax.Precision.HIGH...]
    unnamed x7 -> x0, local copies, waits for them, and re-layouts: 3.6 us -> none
    mul x1 -> x0, local copies, waits for them, and re-layouts: 3.49 us -> none  [per_device(): return mixed * scale_all]
  transfers between devices with their start and end apart: 4 -> 0, of which waited for: 4 -> 0; matrix products, arithmetic and copies ran while one was open for 2% -> 0% of each run, Pallas kernels for 0% -> 0%
where the time goes in v2:
time: 45.4 us; the launch traced here: 45.3 us
  Pallas kernels  45.3 us (100%)
    pallas_call x1, Pallas kernels, gram_call(): pl.pallas_call(functools.partial(gram_kernel, axes, scale), out_shape=(ja...  41.7 us
    pallas_call x1, Pallas kernels, mix_call(): pl.pallas_call(mix_kernel, out_shape=jax.ShapeDtypeStruct(shape, F32), in...  3.57 us

profile of v2, /device:TPU:1, one launch (start us, length us, event | category | flops | bytes accessed | tf_op | source)
XLA Modules:
  0.0 45.3 jit_solution(9998965808077252994)
XLA Ops:
  0.0 41.7 %curl_gram.1 = (f32[8,128]{1,0:T(8,128)S(1)}, bf16[3,8,256,128]{3,2,1,0:T(8,128)(2,1)S(1)}, bf16[3,8,256,128]{3,2,1,0:T(8,128)(2,1)S(1)}, f32[8,8,128]{2,1,0:T(8,128)S(1)}) custom-call(bf16[3,32,8,8,128]{4,3,2,1,0:T(8,128)(2,1)} %vel_hbm.1, f32[8,8,128]{2,1,0:T(8,128)} %weights_hbm.1), custom_call_target="tpu_custom_call" | custom-call | tf_op jit(solution)/shard_map/curl_gram/pallas_call | solution.py:318
  41.7 3.6 %mix.1 = f32[3,32,8,8,128]{4,3,2,1,0:T(8,128)} custom-call(f32[8,128]{1,0:T(8,128)S(1)} %get-tuple-element.9.gram_ref, f32[8,8,128]{2,1,0:T(8,128)S(1)} %get-tuple-element.10.unscale, bf16[3,8,256,128]{3,2,1,0:T(8,128)(2,1)S(1)} %get-tuple-element.11.high, bf16[3,8,256,128]{3,2,1,0:T(8,128)(2,1)S(1)} %get-tuple-element.12.low), custom_call_target="tpu_custom_call" | custom-call | tf_op jit(solution)/shard_map/mix/pallas_call | solution.py:448

commit v3 on v2

--- a/solution.py
+++ b/solution.py
@@ -25,6 +25,7 @@
 
 
 PHASES = (("y", "core"), ("z", "x"))
+ROUNDS = 8
 
 
 def offsets_of(names, dims):
@@ -82,6 +83,7 @@
     z_recv,
     slot_send,
     slot_recv,
+    news,
 ):
     snaps, cells_x, cells_z, cells_y = vel_hbm.shape[1:]
     size = snaps * cells_z
@@ -106,12 +108,31 @@
     right_x, left_x = lax.rem(gx + 1, count_x), lax.rem(gx + count_x - 1, count_x)
     right_z, left_z = lax.rem(gz + 1, count_z), lax.rem(gz + count_z - 1, count_z)
 
+    def beside(*names):
+        return [
+            peer_at((name,), (step,)) for name in names for step in (1, dims[name] - 1) if step
+        ]
+
+    def signal(semaphore, peers):
+        for peer in peers:
+            pl.semaphore_signal(semaphore, inc=1, device_id=peer, device_id_type=MESH)
+
     barrier = pltpu.get_barrier_semaphore()
-    announced = [(right_x, gz), (left_x, gz), (gx, right_z), (gx, left_z)]
-    for names in PHASES:
-        announced += [peer_at(names, offset) for offset in offsets_of(names, dims)]
-    for peer in announced:
-        pl.semaphore_signal(barrier, inc=1, device_id=peer, device_id_type=MESH)
+    direct = [(right_x, gz), (left_x, gz)] + beside("z", "y", "x")
+    signal(barrier, direct)
+    rounds = [beside("x")] * max(dims["x"] // 2 - 1, 0)
+    rounds += [beside("z", "y")] * max(dims["z"] // 2, dims["y"] // 2)
+    heard = [0]
+
+    def tell():
+        if heard[0] < len(rounds):
+            signal(news.at[heard[0]], rounds[heard[0]])
+
+    def hear():
+        if heard[0] < len(rounds):
+            pl.semaphore_wait(news.at[heard[0]], len(rounds[heard[0]]))
+            heard[0] += 1
+            tell()
 
     loads = [
         pltpu.make_async_copy(vel_hbm.at[c], vel.at[c], vel_sem.at[c]) for c in (W, U, V)
@@ -120,7 +141,7 @@
     for load in loads:
         load.start()
 
-    pl.semaphore_wait(barrier, len(announced))
+    pl.semaphore_wait(barrier, len(direct))
 
     z_copies = {}
     x_copies = {}
@@ -159,19 +180,20 @@
     start_z(0)
     start_x()
     start_z(1)
+    tell()
 
     wall = stencil(iota((cells_y, cells_y), 0) - iota((cells_y, cells_y), 1)).astype(BF16)
     wide = (size, size)
     to_row, from_row = iota(wide, 0), iota(wide, 1)
-    same = to_row // cells_z == from_row // cells_z
-    to_z, from_z = lax.rem(to_row, cells_z), lax.rem(from_row, cells_z)
+    to_z, from_z = to_row & (cells_z - 1), from_row & (cells_z - 1)
+    same = to_row - to_z == from_row - from_z
     beyond = jnp.where(from_z < WIDTH, from_z + cells_z, from_z - cells_z)
     for n, source_z in enumerate((from_z, beyond)):
         span_matrix[:, n * size : (n + 1) * size] = jnp.where(
             same, stencil(source_z - to_z), 0.0
         ).astype(BF16)
-    acc[...] = jnp.zeros_like(acc)
-
+
+    hear()
     for load in loads:
         load.wait()
 
@@ -193,10 +215,10 @@
         high[c, x, rows, :] = rounded
         low[c, x, rows, :] = (scaled - rounded.astype(F32)).astype(BF16)
 
-    def accumulate(c, first, count):
+    def product(c, first, count):
         tops = jnp.concatenate([high[c, first + x] for x in range(count)], axis=1)
         rests = jnp.concatenate([low[c, first + x] for x in range(count)], axis=1)
-        acc[...] += dot_nt(jnp.concatenate([tops, rests], axis=0), tops)
+        return dot_nt(jnp.concatenate([tops, rests], axis=0), tops)
 
     rows_pair = PAIR * cells_z
 
@@ -217,6 +239,7 @@
                 total = term if total is None else total + term
             yield x, total.reshape(rows_pair, cells_y)
 
+    hear()
     for side in range(2):
         x_copies[0, side].wait_recv()
 
@@ -226,6 +249,7 @@
         for x, value in stream(0, i):
             keep(2, x, rows, value - part[1, x, rows])
 
+    hear()
     for side in range(2):
         x_copies[1, side].wait_recv()
 
@@ -235,8 +259,9 @@
         for x, value in stream(1, i):
             part[1, x, rows] = value
 
-    for first in range(0, cells_x, 4):
-        accumulate(2, first, 4)
+    hear()
+    acc[...] = product(2, 0, cells_x // 2)
+    acc[...] += product(2, cells_x // 2, cells_x // 2)
 
     for k, source in enumerate((V, U)):
         for first in range(0, cells_x, 2):
@@ -244,19 +269,24 @@
                 z_copies[k, first, side].wait_recv()
             xs = (first, first + 1)
             inner = jnp.concatenate([plane_of(vel, source, x) for x in xs], axis=1)
-            beside = jnp.concatenate([plane_of(halo_z, k, x) for x in xs], axis=1)
-            span = dot_nn(span_matrix[...], jnp.concatenate([inner, beside], axis=0))
+            outer = jnp.concatenate([plane_of(halo_z, k, x) for x in xs], axis=1)
+            span = dot_nn(span_matrix[...], jnp.concatenate([inner, outer], axis=0))
             for n, x in enumerate(xs):
                 cut = span[:, n * cells_y : (n + 1) * cells_y]
                 keep(k, x, slice(None), part[0, x] - cut if k == 0 else cut - part[1, x])
-            accumulate(k, first, 2)
-
-    square = acc[...].reshape(2 * snaps, cells_z, size)
-    match = iota(square.shape, 1) == lax.rem(iota(square.shape, 2), cells_z)
-    matched = jnp.where(match, square, 0.0).sum(axis=1)
+            if k == 0 or first + 2 < cells_x:
+                acc[...] += product(k, first, 2)
+        if k == 0:
+            for _ in range(len(rounds)):
+                hear()
+
+    square = (acc[...] + product(1, cells_x - 2, 2)).reshape(2 * snaps, cells_z, size)
+    match = iota((cells_z, size), 0) == iota((cells_z, size), 1) & (cells_z - 1)
+    matched = jnp.where(match[None], square, 0.0).sum(axis=1)
     matched = 0.5 * matched[:snaps] + matched[snaps:]
     per_row, lanes = gram_ref.shape
-    gather = (iota((size, lanes), 0) // cells_z == iota((size, lanes), 1)).astype(BF16)
+    ahead = iota((size, lanes), 0) - cells_z * iota((size, lanes), 1)
+    gather = ((ahead >= 0) & (ahead < cells_z)).astype(BF16)
     one = matched.astype(BF16)
     rest = matched - one.astype(F32)
     two = rest.astype(BF16)
@@ -341,6 +371,7 @@
             dma((2, cells_x // 2, 2)),
             dma((len(PHASES),)),
             dma((len(PHASES),)),
+            pltpu.SemaphoreType.REGULAR((ROUNDS,)),
         ],
         compiler_params=pltpu.CompilerParams(
             collective_id=0, has_side_effects=True, vmem_limit_bytes=28 << 20
@@ -414,13 +445,13 @@
     place = iota(inverse.shape, 1)
     inverse = jnp.where((place >= snaps) & (place < 2 * snaps), inverse, 0.0)
 
-    spread = (iota((lanes, size), 0) == snaps + iota((lanes, size), 1) // cells_z).astype(BF16)
+    ahead = iota((lanes, size), 1) - cells_z * (iota((lanes, size), 0) - snaps)
+    spread = ((ahead >= 0) & (ahead < cells_z)).astype(BF16)
     top = inverse.astype(BF16)
     rest = (inverse - top.astype(F32)).astype(BF16)
     spans = dot_nn(jnp.concatenate([top, rest], axis=0), spread)
-    cube = (2 * snaps, cells_z, size)
-    match = iota(cube, 1) == lax.rem(iota(cube, 2), cells_z)
-    left = jnp.where(match, jnp.broadcast_to(spans[:, None], cube), 0.0)
+    match = iota((cells_z, size), 0) == iota((cells_z, size), 1) & (cells_z - 1)
+    left = jnp.where(match[None], jnp.broadcast_to(spans[:, None], (2 * snaps, cells_z, size)), 0.0)
     left = left.reshape(2 * size, size).astype(BF16)
 
     stores = []

time: 45.4 us -> 43 us (0.947)
  Pallas kernels: 45.3 us -> 42.9 us
    pallas_call x1, Pallas kernels: 41.7 us -> 39.3 us  [gram_call(): pl.pallas_call(functools.partial(gram_kernel, axes, scale), out_shape=(ja...]
where the time goes in v3:
time: 43 us; the launch traced here: 42.9 us
  Pallas kernels  42.9 us (100%)
    pallas_call x1, Pallas kernels, gram_call(): pl.pallas_call(functools.partial(gram_kernel, axes, scale), out_shape=(ja...  39.3 us
    pallas_call x1, Pallas kernels, mix_call(): pl.pallas_call(mix_kernel, out_shape=jax.ShapeDtypeStruct(shape, F32), in...  3.58 us

profile of v3, /device:TPU:1, one launch (start us, length us, event | category | flops | bytes accessed | tf_op | source)
XLA Modules:
  0.0 42.9 jit_solution(13051040550799694542)
XLA Ops:
  0.0 39.3 %curl_gram.1 = (f32[8,128]{1,0:T(8,128)S(1)}, bf16[3,8,256,128]{3,2,1,0:T(8,128)(2,1)S(1)}, bf16[3,8,256,128]{3,2,1,0:T(8,128)(2,1)S(1)}, f32[8,8,128]{2,1,0:T(8,128)S(1)}) custom-call(bf16[3,32,8,8,128]{4,3,2,1,0:T(8,128)(2,1)} %vel_hbm.1, f32[8,8,128]{2,1,0:T(8,128)} %weights_hbm.1), custom_call_target="tpu_custom_call" | custom-call | tf_op jit(solution)/shard_map/curl_gram/pallas_call | solution.py:348
  39.3 3.6 %mix.1 = f32[3,32,8,8,128]{4,3,2,1,0:T(8,128)} custom-call(f32[8,128]{1,0:T(8,128)S(1)} %get-tuple-element.9.gram_ref, f32[8,8,128]{2,1,0:T(8,128)S(1)} %get-tuple-element.10.unscale, bf16[3,8,256,128]{3,2,1,0:T(8,128)(2,1)S(1)} %get-tuple-element.11.high, bf16[3,8,256,128]{3,2,1,0:T(8,128)(2,1)S(1)} %get-tuple-element.12.low), custom_call_target="tpu_custom_call" | custom-call | tf_op jit(solution)/shard_map/mix/pallas_call | solution.py:479

commit v4 on v3

--- a/solution.py
+++ b/solution.py
@@ -280,10 +280,10 @@
             for _ in range(len(rounds)):
                 hear()
 
-    square = (acc[...] + product(1, cells_x - 2, 2)).reshape(2 * snaps, cells_z, size)
+    square = acc[...] + product(1, cells_x - 2, 2)
+    square = (0.5 * square[:size] + square[size:]).reshape(snaps, cells_z, size)
     match = iota((cells_z, size), 0) == iota((cells_z, size), 1) & (cells_z - 1)
     matched = jnp.where(match[None], square, 0.0).sum(axis=1)
-    matched = 0.5 * matched[:snaps] + matched[snaps:]
     per_row, lanes = gram_ref.shape
     ahead = iota((size, lanes), 0) - cells_z * iota((size, lanes), 1)
     gather = ((ahead >= 0) & (ahead < cells_z)).astype(BF16)
@@ -380,41 +380,41 @@
     )(velocity, weights)
 
 
-BLOCK = 8
-
-
-def eliminate(gram):
-    snaps, lanes = gram.shape
-    tile = 8
-    lane = iota((tile, lanes), 1)
-    row = iota((tile, lanes), 0)
-    full = (tile, lanes)
-    work = []
-    for t in range(snaps // tile):
-        unit = jnp.where(lane == row + snaps + t * tile, 1.0, 0.0)
-        work.append(jnp.where(lane < snaps, gram[t * tile : (t + 1) * tile], unit))
-    roots = [jnp.ones(full, F32) for _ in work]
-    for b in range(0, snaps, BLOCK):
-        steps = range(BLOCK)
-        home, at = b // tile, [(b + j) % tile for j in steps]
-        rows = [jnp.broadcast_to(work[home][at[j] : at[j] + 1], full) for j in steps]
-        columns = [
-            {
-                t: jnp.broadcast_to(work[t][:, b + j : b + j + 1], full)
-                for t in range(home, len(work))
-            }
-            for j in steps
-        ]
+TILE = 8
+
+
+class Elimination:
+    def __init__(self, gram):
+        snaps, lanes = gram.shape
+        self.full = (TILE, lanes)
+        lane = iota(self.full, 1)
+        self.row = iota(self.full, 0)
+        self.inside = (lane >= snaps) & (lane < 2 * snaps)
+        self.work = []
+        for t in range(snaps // TILE):
+            unit = jnp.where(lane == self.row + snaps + t * TILE, 1.0, 0.0)
+            self.work.append(jnp.where(lane < snaps, gram[t * TILE : (t + 1) * TILE], unit))
+        self.pivots = [jnp.ones(self.full, F32) for _ in self.work]
+
+    def sweep(self, home, between):
+        work, full = self.work, self.full
+        steps = range(TILE)
+        rows = [jnp.broadcast_to(work[home][j : j + 1], full) for j in steps]
+        columns = []
+        for j in steps:
+            k = home * TILE + j
+            columns.append(
+                {t: jnp.broadcast_to(work[t][:, k : k + 1], full) for t in range(home, len(work))}
+            )
         cross = [
-            [jnp.broadcast_to(columns[j][home][at[i] : at[i] + 1], full) for j in steps]
-            for i in steps
+            [jnp.broadcast_to(columns[j][home][i : i + 1], full) for j in steps] for i in steps
         ]
         for j in steps:
             pivot = cross[j][j]
             inverse = 1.0 / pivot
-            roots[home] = jnp.where(row == at[j], pivot, roots[home])
+            self.pivots[home] = jnp.where(self.row == j, pivot, self.pivots[home])
             factors = {t: columns[j][t] * inverse for t in columns[j]}
-            factors[home] = jnp.where(row > at[j], factors[home], 0.0)
+            factors[home] = jnp.where(self.row > j, factors[home], 0.0)
             for m in steps[j + 1 :]:
                 for t in columns[m]:
                     columns[m][t] = columns[m][t] - factors[t] * cross[j][m]
@@ -425,52 +425,90 @@
                     cross[i][m] = cross[i][m] - ratio * cross[j][m]
             for t in columns[j]:
                 work[t] = work[t] - factors[t] * rows[j]
-    return jnp.concatenate([w / jnp.sqrt(r) for w, r in zip(work, roots, strict=True)], axis=0)
+            between()
+
+    def rows_of(self, tiles):
+        return jnp.concatenate(
+            [
+                jnp.where(self.inside, self.work[t] / jnp.sqrt(self.pivots[t]), 0.0)
+                for t in tiles
+            ],
+            axis=0,
+        )
 
 
 def mix_kernel(gram_ref, unscale, high, low, out_hbm, out, out_sem):
     _, cells_x, size, cells_y = high.shape
     snaps = out.shape[1]
     cells_z = size // snaps
+    half = size // 2
 
     packed = gram_ref[...]
     lanes = packed.shape[1]
     pieces = [packed] + [
         pltpu.roll(packed, lanes - q * snaps, 1) for q in range(1, lanes // snaps)
     ]
-    half = jnp.concatenate(pieces, axis=0)
-    half = jnp.where(iota(half.shape, 1) < snaps, half, 0.0)
-    tall = jnp.concatenate([half, jnp.zeros((lanes - snaps, lanes), F32)], axis=0)
-    inverse = eliminate(half + tall.T[:snaps])
-    place = iota(inverse.shape, 1)
-    inverse = jnp.where((place >= snaps) & (place < 2 * snaps), inverse, 0.0)
+    part = jnp.concatenate(pieces, axis=0)
+    part = jnp.where(iota(part.shape, 1) < snaps, part, 0.0)
+    tall = jnp.concatenate([part, jnp.zeros((lanes - snaps, lanes), F32)], axis=0)
+    work = Elimination(part + tall.T[:snaps])
 
     ahead = iota((lanes, size), 1) - cells_z * (iota((lanes, size), 0) - snaps)
     spread = ((ahead >= 0) & (ahead < cells_z)).astype(BF16)
-    top = inverse.astype(BF16)
-    rest = (inverse - top.astype(F32)).astype(BF16)
-    spans = dot_nn(jnp.concatenate([top, rest], axis=0), spread)
     match = iota((cells_z, size), 0) == iota((cells_z, size), 1) & (cells_z - 1)
-    left = jnp.where(match[None], jnp.broadcast_to(spans[:, None], (2 * snaps, cells_z, size)), 0.0)
-    left = left.reshape(2 * size, size).astype(BF16)
-
+
+    def blocks(rows, columns):
+        top = rows.astype(BF16)
+        rest = (rows - top.astype(F32)).astype(BF16)
+        spans = dot_nn(jnp.concatenate([top, rest], axis=0), spread[:, :columns])
+        cube = (2 * rows.shape[0], cells_z, columns)
+        wide = jnp.where(match[None, :, :columns], jnp.broadcast_to(spans[:, None], cube), 0.0)
+        return wide.reshape(-1, columns).astype(BF16)
+
+    pairs = [(c, first) for c in range(3) for first in range(0, cells_x, 2)]
     stores = []
-    for c in range(3):
-        for first in range(0, cells_x, 2):
-            xs = (first, first + 1)
-            a = jnp.concatenate([high[c, x] for x in xs], axis=1)
-            b = jnp.concatenate([low[c, x] for x in xs], axis=1)
-            mixed = dot_nn(left, a)
-            mixed = mixed[:size] + mixed[size:] + dot_nn(left[:size], b)
-            for n, x in enumerate(xs):
-                cut = mixed[:, n * cells_y : (n + 1) * cells_y]
-                out[c, :, x] = cut.reshape(snaps, cells_z, cells_y) * unscale[x][None]
-            where = (c, slice(None), pl.ds(first, 2))
-            copy = pltpu.make_async_copy(
-                out.at[where], out_hbm.at[where], out_sem.at[c, first // 2]
-            )
-            copy.start()
-            stores.append(copy)
+
+    def sides(ref, c, first, rows):
+        return jnp.concatenate([ref[c, first + n, :rows] for n in range(2)], axis=1)
+
+    def put(c, first, begin, mixed):
+        count = mixed.shape[0] // cells_z
+        for n in range(2):
+            cut = mixed[:, n * cells_y : (n + 1) * cells_y]
+            cut = cut.reshape(count, cells_z, cells_y) * unscale[first + n][None]
+            out[c, begin : begin + count, first + n] = cut
+
+    def send(where, semaphore):
+        copy = pltpu.make_async_copy(out.at[where], out_hbm.at[where], semaphore)
+        copy.start()
+        stores.append(copy)
+
+    for home in range(2):
+        work.sweep(home, lambda: None)
+    first_rows = blocks(work.rows_of((0, 1)), half)
+    twice = jnp.concatenate([first_rows[:half]] * 2, axis=1)
+    todo = list(pairs)
+
+    def early():
+        if todo:
+            c, first = todo.pop(0)
+            a, b = sides(high, c, first, half), sides(low, c, first, half)
+            mixed = dot_nn(twice, jnp.concatenate([a, b], axis=0)) + dot_nn(first_rows[half:], a)
+            put(c, first, 0, mixed)
+            if first + 2 == cells_x:
+                send((c, pl.ds(0, snaps // 2)), out_sem.at[0, c])
+
+    for home in range(2, 4):
+        work.sweep(home, early)
+    while todo:
+        early()
+    second_rows = blocks(work.rows_of((2, 3)), size)
+    for n, (c, first) in enumerate(pairs):
+        mixed = dot_nn(second_rows, sides(high, c, first, size))
+        mixed = mixed[:half] + mixed[half:]
+        mixed += dot_nn(second_rows[:half], sides(low, c, first, size))
+        put(c, first, snaps // 2, mixed)
+        send((c, pl.ds(snaps // 2, snaps // 2), pl.ds(first, 2)), out_sem.at[1, n])
     for copy in stores:
         copy.wait()
 
@@ -483,7 +521,7 @@
         out_specs=pl.BlockSpec(memory_space=pltpu.HBM),
         scratch_shapes=[
             pltpu.VMEM(shape, F32),
-            pltpu.SemaphoreType.DMA((3, shape[2] // 2)),
+            pltpu.SemaphoreType.DMA((2, 3 * shape[2] // 2)),
         ],
         compiler_params=pltpu.CompilerParams(vmem_limit_bytes=28 << 20),
         name="mix",

time: 43 us -> 42.4 us (0.986)
  Pallas kernels: 42.9 us -> 42.3 us
    pallas_call x1, Pallas kernels: 3.58 us -> 3.07 us  [mix_call(): pl.pallas_call(mix_kernel, out_shape=jax.ShapeDtypeStruct(shape, F32), in...]
where the time goes in v4:
time: 42.4 us; the launch traced here: 42.3 us
  Pallas kernels  42.3 us (100%)
    pallas_call x1, Pallas kernels, gram_call(): pl.pallas_call(functools.partial(gram_kernel, axes, scale), out_shape=(ja...  39.3 us
    pallas_call x1, Pallas kernels, mix_call(): pl.pallas_call(mix_kernel, out_shape=jax.ShapeDtypeStruct(shape, F32), in...  3.07 us

profile of v4, /device:TPU:1, one launch (start us, length us, event | category | flops | bytes accessed | tf_op | source)
XLA Modules:
  0.0 42.3 jit_solution(10203371609863806747)
XLA Ops:
  0.0 39.3 %curl_gram.1 = (f32[8,128]{1,0:T(8,128)S(1)}, bf16[3,8,256,128]{3,2,1,0:T(8,128)(2,1)S(1)}, bf16[3,8,256,128]{3,2,1,0:T(8,128)(2,1)S(1)}, f32[8,8,128]{2,1,0:T(8,128)S(1)}) custom-call(bf16[3,32,8,8,128]{4,3,2,1,0:T(8,128)(2,1)} %vel_hbm.1, f32[8,8,128]{2,1,0:T(8,128)} %weights_hbm.1), custom_call_target="tpu_custom_call" | custom-call | tf_op jit(solution)/shard_map/curl_gram/pallas_call | solution.py:348
  39.3 3.1 %mix.1 = f32[3,32,8,8,128]{4,3,2,1,0:T(8,128)} custom-call(f32[8,128]{1,0:T(8,128)S(1)} %get-tuple-element.9.gram_ref, f32[8,8,128]{2,1,0:T(8,128)S(1)} %get-tuple-element.10.unscale, bf16[3,8,256,128]{3,2,1,0:T(8,128)(2,1)S(1)} %get-tuple-element.11.high, bf16[3,8,256,128]{3,2,1,0:T(8,128)(2,1)S(1)} %get-tuple-element.12.low), custom_call_target="tpu_custom_call" | custom-call | tf_op jit(solution)/shard_map/mix/pallas_call | solution.py:517

commit v5 on v4

--- a/solution.py
+++ b/solution.py
@@ -24,7 +24,7 @@
     return {"y": count_x // (core * x), "x": x, "core": core, "z": count_z}
 
 
-PHASES = (("y", "core"), ("z", "x"))
+PHASES = (("z", "core"), ("y", "x"))
 ROUNDS = 8
 
 
@@ -145,18 +145,20 @@
 
     z_copies = {}
     x_copies = {}
+    twos = [(first, 2) for first in range(0, cells_x, 2)]
+    chunks = ([(0, 4), (4, 4)], [(0, 4), (4, 2), (6, 2)])
 
     def start_z(k):
         source = (V, U)[k]
-        for first in range(0, cells_x, 2):
-            xs = pl.ds(first, 2)
+        for first, count in chunks[k]:
+            xs = pl.ds(first, count)
             for side, peer in ((0, (gx, left_z)), (1, (gx, right_z))):
                 rows = pl.ds(side * WIDTH, WIDTH)
                 copy = pltpu.make_async_remote_copy(
                     src_ref=vel_hbm.at[source, :, xs, rows, :],
                     dst_ref=halo_z.at[k, :, xs, rows, :],
-                    send_sem=z_send.at[k, first // 2, side],
-                    recv_sem=z_recv.at[k, first // 2, side],
+                    send_sem=z_send.at[k, first, side],
+                    recv_sem=z_recv.at[k, first, side],
                     device_id=peer,
                     device_id_type=MESH,
                 )
@@ -264,23 +266,23 @@
     acc[...] += product(2, cells_x // 2, cells_x // 2)
 
     for k, source in enumerate((V, U)):
-        for first in range(0, cells_x, 2):
+        for first, count in chunks[k]:
             for side in range(2):
                 z_copies[k, first, side].wait_recv()
-            xs = (first, first + 1)
+            xs = range(first, first + count)
             inner = jnp.concatenate([plane_of(vel, source, x) for x in xs], axis=1)
             outer = jnp.concatenate([plane_of(halo_z, k, x) for x in xs], axis=1)
             span = dot_nn(span_matrix[...], jnp.concatenate([inner, outer], axis=0))
             for n, x in enumerate(xs):
                 cut = span[:, n * cells_y : (n + 1) * cells_y]
                 keep(k, x, slice(None), part[0, x] - cut if k == 0 else cut - part[1, x])
-            if k == 0 or first + 2 < cells_x:
-                acc[...] += product(k, first, 2)
+            if (k, first, count) != (1, *chunks[1][-1]):
+                acc[...] += product(k, first, count)
         if k == 0:
             for _ in range(len(rounds)):
                 hear()
 
-    square = acc[...] + product(1, cells_x - 2, 2)
+    square = acc[...] + product(1, *chunks[1][-1])
     square = (0.5 * square[:size] + square[size:]).reshape(snaps, cells_z, size)
     match = iota((cells_z, size), 0) == iota((cells_z, size), 1) & (cells_z - 1)
     matched = jnp.where(match[None], square, 0.0).sum(axis=1)
@@ -367,8 +369,8 @@
             dma((4,)),
             dma((2, 2)),
             dma((2, 2)),
-            dma((2, cells_x // 2, 2)),
-            dma((2, cells_x // 2, 2)),
+            dma((2, cells_x, 2)),
+            dma((2, cells_x, 2)),
             dma((len(PHASES),)),
             dma((len(PHASES),)),
             pltpu.SemaphoreType.REGULAR((ROUNDS,)),

time: 42.4 us -> 42.1 us (level)
  no operation moved by 1% of the time
where the time goes in v5:
time: 42.1 us; the launch traced here: 42 us
  Pallas kernels  42 us (100%)
    pallas_call x1, Pallas kernels, gram_call(): pl.pallas_call(functools.partial(gram_kernel, axes, scale), out_shape=(ja...  38.9 us
    pallas_call x1, Pallas kernels, mix_call(): pl.pallas_call(mix_kernel, out_shape=jax.ShapeDtypeStruct(shape, F32), in...  3.07 us

profile of v5, /device:TPU:1, one launch (start us, length us, event | category | flops | bytes accessed | tf_op | source)
XLA Modules:
  0.0 42.0 jit_solution(6992917139774591112)
XLA Ops:
  0.0 38.9 %curl_gram.1 = (f32[8,128]{1,0:T(8,128)S(1)}, bf16[3,8,256,128]{3,2,1,0:T(8,128)(2,1)S(1)}, bf16[3,8,256,128]{3,2,1,0:T(8,128)(2,1)S(1)}, f32[8,8,128]{2,1,0:T(8,128)S(1)}) custom-call(bf16[3,32,8,8,128]{4,3,2,1,0:T(8,128)(2,1)} %vel_hbm.1, f32[8,8,128]{2,1,0:T(8,128)} %weights_hbm.1), custom_call_target="tpu_custom_call" | custom-call | tf_op jit(solution)/shard_map/curl_gram/pallas_call | solution.py:350
  38.9 3.1 %mix.1 = f32[3,32,8,8,128]{4,3,2,1,0:T(8,128)} custom-call(f32[8,128]{1,0:T(8,128)S(1)} %get-tuple-element.9.gram_ref, f32[8,8,128]{2,1,0:T(8,128)S(1)} %get-tuple-element.10.unscale, bf16[3,8,256,128]{3,2,1,0:T(8,128)(2,1)S(1)} %get-tuple-element.11.high, bf16[3,8,256,128]{3,2,1,0:T(8,128)(2,1)S(1)} %get-tuple-element.12.low), custom_call_target="tpu_custom_call" | custom-call | tf_op jit(solution)/shard_map/mix/pallas_call | solution.py:519

commit v6 on v5

--- a/solution.py
+++ b/solution.py
@@ -75,6 +75,7 @@
     part,
     span_matrix,
     acc,
+    gather,
     slots,
     vel_sem,
     x_send,
@@ -213,13 +214,14 @@
 
     def keep(c, x, rows, value):
         scaled = (value.reshape(-1, cells_z, cells_y) * root[x][None]).reshape(value.shape)
-        rounded = scaled.astype(BF16)
-        high[c, x, rows, :] = rounded
-        low[c, x, rows, :] = (scaled - rounded.astype(F32)).astype(BF16)
-
-    def product(c, first, count):
-        tops = jnp.concatenate([high[c, first + x] for x in range(count)], axis=1)
-        rests = jnp.concatenate([low[c, first + x] for x in range(count)], axis=1)
+        top = scaled.astype(BF16)
+        rest = (scaled - top.astype(F32)).astype(BF16)
+        high[c, x, rows, :] = top
+        low[c, x, rows, :] = rest
+        return top, rest
+
+    def product(planes):
+        tops, rests = (jnp.concatenate(side, axis=1) for side in zip(*planes, strict=True))
         return dot_nt(jnp.concatenate([tops, rests], axis=0), tops)
 
     rows_pair = PAIR * cells_z
@@ -262,8 +264,11 @@
             part[1, x, rows] = value
 
     hear()
-    acc[...] = product(2, 0, cells_x // 2)
-    acc[...] += product(2, cells_x // 2, cells_x // 2)
+    kept = [(high[2, x], low[2, x]) for x in range(cells_x)]
+    acc[...] = product(kept[: cells_x // 2])
+    acc[...] += product(kept[cells_x // 2 :])
+    ahead = iota(gather.shape, 0) - cells_z * iota(gather.shape, 1)
+    gather[...] = ((ahead >= 0) & (ahead < cells_z)).astype(BF16)
 
     for k, source in enumerate((V, U)):
         for first, count in chunks[k]:
@@ -273,27 +278,27 @@
             inner = jnp.concatenate([plane_of(vel, source, x) for x in xs], axis=1)
             outer = jnp.concatenate([plane_of(halo_z, k, x) for x in xs], axis=1)
             span = dot_nn(span_matrix[...], jnp.concatenate([inner, outer], axis=0))
+            kept = []
             for n, x in enumerate(xs):
                 cut = span[:, n * cells_y : (n + 1) * cells_y]
-                keep(k, x, slice(None), part[0, x] - cut if k == 0 else cut - part[1, x])
+                value = part[0, x] - cut if k == 0 else cut - part[1, x]
+                kept.append(keep(k, x, slice(None), value))
             if (k, first, count) != (1, *chunks[1][-1]):
-                acc[...] += product(k, first, count)
+                acc[...] += product(kept)
         if k == 0:
             for _ in range(len(rounds)):
                 hear()
 
-    square = acc[...] + product(1, *chunks[1][-1])
+    square = acc[...] + product(kept)
     square = (0.5 * square[:size] + square[size:]).reshape(snaps, cells_z, size)
     match = iota((cells_z, size), 0) == iota((cells_z, size), 1) & (cells_z - 1)
     matched = jnp.where(match[None], square, 0.0).sum(axis=1)
-    per_row, lanes = gram_ref.shape
-    ahead = iota((size, lanes), 0) - cells_z * iota((size, lanes), 1)
-    gather = ((ahead >= 0) & (ahead < cells_z)).astype(BF16)
+    per_row = gram_ref.shape[0]
     one = matched.astype(BF16)
     rest = matched - one.astype(F32)
     two = rest.astype(BF16)
     three = (rest - two.astype(F32)).astype(BF16)
-    half = dot_nn(jnp.concatenate([one, two, three], axis=0), gather)
+    half = dot_nn(jnp.concatenate([one, two, three], axis=0), gather[...])
     half = half[:snaps] + half[snaps : 2 * snaps] + half[2 * snaps :]
     packed = half[:per_row]
     for q in range(1, snaps // per_row):
@@ -365,6 +370,7 @@
             pltpu.VMEM((2, cells_x, size, cells_y), F32),
             pltpu.VMEM((size, 2 * size), BF16),
             pltpu.VMEM((2 * size, size), F32),
+            pltpu.VMEM((size, 128), BF16),
             pltpu.VMEM((tiles, 8, 128), F32),
             dma((4,)),
             dma((2, 2)),

time: 42.1 us -> 42.1 us (level)
  no operation moved by 1% of the time
where the time goes in v6:
time: 42.1 us; the launch traced here: 42 us
  Pallas kernels  42 us (100%)
    pallas_call x1, Pallas kernels, gram_call(): pl.pallas_call(functools.partial(gram_kernel, axes, scale), out_shape=(ja...  38.9 us
    pallas_call x1, Pallas kernels, mix_call(): pl.pallas_call(mix_kernel, out_shape=jax.ShapeDtypeStruct(shape, F32), in...  3.07 us

profile of v6, /device:TPU:1, one launch (start us, length us, event | category | flops | bytes accessed | tf_op | source)
XLA Modules:
  0.0 42.0 jit_solution(8982728602012197816)
XLA Ops:
  0.0 38.9 %curl_gram.1 = (f32[8,128]{1,0:T(8,128)S(1)}, bf16[3,8,256,128]{3,2,1,0:T(8,128)(2,1)S(1)}, bf16[3,8,256,128]{3,2,1,0:T(8,128)(2,1)S(1)}, f32[8,8,128]{2,1,0:T(8,128)S(1)}) custom-call(bf16[3,32,8,8,128]{4,3,2,1,0:T(8,128)(2,1)} %vel_hbm.1, f32[8,8,128]{2,1,0:T(8,128)} %weights_hbm.1), custom_call_target="tpu_custom_call" | custom-call | tf_op jit(solution)/shard_map/curl_gram/pallas_call | solution.py:355
  38.9 3.1 %mix.1 = f32[3,32,8,8,128]{4,3,2,1,0:T(8,128)} custom-call(f32[8,128]{1,0:T(8,128)S(1)} %get-tuple-element.9.gram_ref, f32[8,8,128]{2,1,0:T(8,128)S(1)} %get-tuple-element.10.unscale, bf16[3,8,256,128]{3,2,1,0:T(8,128)(2,1)S(1)} %get-tuple-element.11.high, bf16[3,8,256,128]{3,2,1,0:T(8,128)(2,1)S(1)} %get-tuple-element.12.low), custom_call_target="tpu_custom_call" | custom-call | tf_op jit(solution)/shard_map/mix/pallas_call | solution.py:525
